TPU v7x, 128 devices: a whole 4x4x4 slice. The times are simulated.
128 devices in a mesh: expert: 4 (over y), blk: 32 (over z, x, core).
Axes of the slice: x: 4, y: 4, z: 4, core: 2. Of those that a mesh axis runs over, the one named last changes fastest.
Arguments:
- tokens: bfloat16 [2, 512, 6144], P(None, 'expert', 'blk'), may hold values from -6 to 6
- expert_ids: int32 [2, 512, 2], P(None, 'expert'), may hold values from 0 to 3, all different within a row; in each aligned block of 128 rows (0 to 127, 128 to 255, ..., all dimensions but the last counted through in order) at most 128 rows name the same one
- route_share: float32 [2, 512], P(None, 'expert'), may hold values from 0.1 to 0.9
- gate_weight: bfloat16 [4, 6144, 16384], P('expert', None, 'blk'), may hold values from -0.078125 to 0.078125
- up_weight: bfloat16 [4, 6144, 16384], P('expert', None, 'blk'), may hold values from -0.078125 to 0.078125
- down_weight: bfloat16 [4, 16384, 6144], P('expert', 'blk'), may hold values from -0.09375 to 0.09375
Outputs:
- combined: bfloat16 [2, 512, 6144], P(None, 'expert', 'blk')
Inputs may be any that keep to these rules, and one draw needn't show every extreme that they name: `expert_ids`: each row names two different experts.
All inputs are finite; a program needn't handle non-finite values.
Results may differ from a plain program's by a relative error of at most 0.023.
Values may be sent and summed in bfloat16 or wider, within the bound.
No kernel may reach another device: no remote copies, remote signals or barrier semaphores. Data moves between devices by JAX's collectives and lax.ppermute only.
A program may use at most 128 MiB of HBM per device.

v0:
```python
import jax
import jax.numpy as jnp
from jax import lax
from jax.sharding import PartitionSpec as P


def routing(expert_ids, route_share, experts):
    row_count = expert_ids.shape[1]
    labels = jnp.arange(experts, dtype=jnp.int32)
    first_hit = (expert_ids[:, :, 0:1] == labels).astype(jnp.float32)
    second = (expert_ids[:, :, 1:2] == labels).astype(jnp.float32)
    chosen = first_hit + second
    weight = route_share[:, :, None] * first_hit + (1.0 - route_share[:, :, None]) * second
    slot_pos = jnp.cumsum(chosen.astype(jnp.int32), axis=1) - 1
    slot_ids = jnp.arange(row_count, dtype=jnp.int32)
    placed = ((slot_pos[:, :, :, None] == slot_ids) & (chosen[:, :, :, None] > 0)).astype(
        jnp.bfloat16
    )
    return (placed, weight)


def expert_layer(tokens, expert_ids, route_share, gate_mat, up_mat, down_mat, experts):
    step_count, row_count, feature_cols = tokens.shape
    placed, weight = routing(expert_ids, route_share, experts)
    outgoing = jnp.einsum(
        "gres,grd->gesd", placed, tokens, preferred_element_type=jnp.float32
    ).astype(jnp.bfloat16)
    arrived = lax.all_to_all(outgoing, "expert", split_axis=1, concat_axis=1, tiled=True)
    slot_rows = arrived.reshape(-1, feature_cols)
    fragment = lax.all_gather(slot_rows, "blk", axis=1, tiled=True)
    gate_pre = jnp.dot(fragment, gate_mat, preferred_element_type=jnp.float32)
    up_pre = jnp.dot(fragment, up_mat, preferred_element_type=jnp.float32)
    hidden = (jax.nn.silu(gate_pre) * up_pre).astype(jnp.bfloat16)
    summed = lax.psum_scatter(
        lax.dot_general(
            down_mat, hidden, (((0,), (1,)), ((), ())), preferred_element_type=jnp.float32
        ).astype(jnp.bfloat16),
        "blk",
        scatter_dimension=0,
        tiled=True,
    )
    returned = lax.all_to_all(
        summed.reshape(feature_cols, step_count, experts, row_count),
        "expert",
        split_axis=2,
        concat_axis=2,
        tiled=True,
    )
    picked = jnp.einsum("gres,dges->gerd", placed, returned, preferred_element_type=jnp.float32)
    combined = jnp.sum(jnp.transpose(weight, (0, 2, 1))[:, :, :, None] * picked, axis=1)
    return combined.astype(jnp.bfloat16)


def body(tokens, expert_ids, route_share, gate_weight, up_weight, down_weight):
    experts = lax.axis_size("expert")
    gate_mat = gate_weight[0]
    up_mat = up_weight[0]
    down_mat = down_weight[0]
    results = []
    for step_idx in range(tokens.shape[0]):
        results.append(
            expert_layer(
                tokens[step_idx : step_idx + 1],
                expert_ids[step_idx : step_idx + 1],
                route_share[step_idx : step_idx + 1],
                gate_mat,
                up_mat,
                down_mat,
                experts,
            )
        )
    return jnp.concatenate(results, axis=0)


def solution(mesh):
    return jax.shard_map(
        body,
        mesh=mesh,
        in_specs=(
            P(None, "expert", "blk"),
            P(None, "expert", None),
            P(None, "expert"),
            P("expert", None, "blk"),
            P("expert", None, "blk"),
            P("expert", "blk", None),
        ),
        out_specs=P(None, "expert", "blk"),
        check_vma=False,
    )
```

profile of v0, /device:TPU:0, one launch (start us, length us, event | category | flops | bytes accessed | tf_op | source)
XLA Modules:
  0.0 319.7 jit_solution(13525887074447122003)
XLA Ops:
  6.5 0.8 slice_bitcast_fusion.5
  7.9 1.2 fusion.26
  9.1 10.7 %all_to_all.20 = bf16[1,4,128,192]{2,3,0,1:T(8,128)(2,1)S(1)} all-to-all(bf16[1,4,128,192]{2,3,0,1:T(8,128)(2,1)S(1)} %fusion.26), channel_id=1, replica_groups=mesh['expert'=4,'blk'=32] {'expert'}, dimensions={1} | all-to-all | bytes 393216 | tf_op jit(solution)/shard_map/all_to_all | solution.py:28
  20.0 0.7 copy.40
  20.7 0.2 reduce_window_sum.18
  21.1 1.2 fusion.27
  22.3 8.7 %all_to_all.21 = bf16[1,4,128,192]{2,3,0,1:T(8,128)(2,1)S(1)} all-to-all(bf16[1,4,128,192]{2,3,0,1:T(8,128)(2,1)S(1)} %fusion.27), channel_id=1, replica_groups=mesh['expert'=4,'blk'=32] {'expert'}, dimensions={1} | all-to-all | bytes 393216 | tf_op jit(solution)/shard_map/all_to_all | solution.py:28
  31.1 0.7 copy.39
  31.9 38.5 %all-gather.3.cloned.1.call-done = bf16[512,6144]{0,1:T(8,128)(2,1)} async-done(((bf16[512,192]{0,1:T(8,128)(2,1)}), bf16[512,6144]{0,1:T(8,128)(2,1)}) %all-gather.3.cloned.1.call-update) | async-done | bytes 6291472 | tf_op jit(solution)/shard_map/all_gather | solution.py:30
  70.5 8.2 %fusion.10 = f32[512,512]{1,0:T(8,128)S(1)} fusion(bf16[512,6144]{0,1:T(8,128)(2,1)} %all-gather.3.cloned.1.call-done, bf16[1,6144,512]{2,1,0:T(8,128)(2,1)} %param.9), kind=kOutput, calls=%fused_computation.12 | convolution fusion | flops 3221225472 | bytes 13631488 | tf_op jit(solution)/shard_map/dot_general | solution.py:31
  78.7 6.5 %fusion.21 = bf16[512,512]{1,0:T(8,128)(2,1)S(1)} fusion(bf16[512,6144]{0,1:T(8,128)(2,1)S(1)} %copy-done.1, bf16[1,6144,512]{2,1,0:T(8,128)(2,1)} %param.10, f32[512,512]{1,0:T(8,128)S(1)} %fusion.10), kind=kOutput, calls=%fused_computation.17 | convolution fusion | flops 3222798336 | bytes 14155776 | tf_op jit(solution)/shard_map/dot_general | solution.py:32
  85.2 5.3 %fusion = bf16[6144,512]{0,1:T(8,128)(2,1)} fusion(bf16[512,512]{1,0:T(8,128)(2,1)S(1)} %fusion.21, bf16[1,512,6144]{2,1,0:T(8,128)(2,1)S(1)} %bitcast.112), kind=kOutput, calls=%fused_computation.2 | convolution fusion | flops 3224371200 | bytes 13107200 | tf_op jit(solution)/shard_map/dot_general | solution.py:35
  90.5 8.7 %copy.31 = bf16[6144,512]{1,0:T(8,128)(2,1)} copy(bf16[6144,512]{0,1:T(8,128)(2,1)} %fusion) | data formatting | bytes 12582912
  99.2 0.2 reduce-scatter.9.cloned.1.call-start
  99.4 21.5 %all-gather.5.cloned.1.call-done = bf16[512,6144]{0,1:T(8,128)(2,1)} async-done(((bf16[512,192]{0,1:T(8,128)(2,1)}), bf16[512,6144]{0,1:T(8,128)(2,1)}) %all-gather.5.cloned.1.call-update) | async-done | bytes 6291472 | tf_op jit(solution)/shard_map/all_gather | solution.py:30
  120.9 8.2 %fusion.8 = f32[512,512]{1,0:T(8,128)S(1)} fusion(bf16[512,6144]{0,1:T(8,128)(2,1)} %all-gather.5.cloned.1.call-done, bf16[1,6144,512]{2,1,0:T(8,128)(2,1)} %param.9), kind=kOutput, calls=%fused_computation.10 | convolution fusion | flops 3221225472 | bytes 13631488 | tf_op jit(solution)/shard_map/dot_general | solution.py:31
  129.1 6.5 %fusion.18 = bf16[512,512]{1,0:T(8,128)(2,1)S(1)} fusion(bf16[512,6144]{0,1:T(8,128)(2,1)S(1)} %copy-done.2, bf16[1,6144,512]{2,1,0:T(8,128)(2,1)} %param.10, f32[512,512]{1,0:T(8,128)S(1)} %fusion.8), kind=kOutput, calls=%fused_computation.16 | convolution fusion | flops 3222798336 | bytes 14155776 | tf_op jit(solution)/shard_map/dot_general | solution.py:32
  135.7 5.3 %fusion.1 = bf16[6144,512]{0,1:T(8,128)(2,1)} fusion(bf16[512,512]{1,0:T(8,128)(2,1)S(1)} %fusion.18, bf16[1,512,6144]{2,1,0:T(8,128)(2,1)S(1)} %bitcast.114), kind=kOutput, calls=%fused_computation.3 | convolution fusion | flops 3224371200 | bytes 13107200 | tf_op jit(solution)/shard_map/dot_general | solution.py:35
  141.0 8.8 %copy.33 = bf16[6144,512]{1,0:T(8,128)(2,1)} copy(bf16[6144,512]{0,1:T(8,128)(2,1)} %fusion.1) | data formatting | bytes 12582912
  149.8 0.7 copy-done
  150.5 59.4 %reduce-scatter.7.cloned.1.call-done = bf16[192,512]{1,0:T(8,128)(2,1)} async-done(((bf16[6144,512]{1,0:T(8,128)(2,1)}), bf16[192,512]{1,0:T(8,128)(2,1)}) %reduce-scatter.7.cloned.1.call-update) | async-done | bytes 196624
  209.9 1.1 copy.32
  211.0 0.8 copy.25
  211.8 4.3 %all-to-all-start.1 = ((bf16[192,1,4,128]{3,0,1,2:T(8,128)(2,1)}), bf16[192,1,4,128]{3,0,1,2:T(8,128)(2,1)S(1)}, u32[]{:S(2)}, u32[]{:S(2)}) async-start(bf16[192,1,4,128]{3,0,1,2:T(8,128)(2,1)} %copy.25), calls=%async_computation.1 | async-start | bytes 393216 | tf_op jit(solution)/shard_map/all_to_all | solution.py:42
  216.1 83.5 %reduce-scatter.9.cloned.1.call-done = bf16[192,512]{1,0:T(8,128)(2,1)} async-done(((bf16[6144,512]{1,0:T(8,128)(2,1)}), bf16[192,512]{1,0:T(8,128)(2,1)}) %reduce-scatter.9.cloned.1.call-update) | async-done | bytes 196624
  299.6 1.1 copy.34
  300.7 0.8 copy.30
  301.5 4.3 %all-to-all-start.3 = ((bf16[192,1,4,128]{3,0,1,2:T(8,128)(2,1)}), bf16[192,1,4,128]{3,0,1,2:T(8,128)(2,1)S(1)}, u32[]{:S(2)}, u32[]{:S(2)}) async-start(bf16[192,1,4,128]{3,0,1,2:T(8,128)(2,1)} %copy.30), calls=%async_computation.3 | async-start | bytes 393216 | tf_op jit(solution)/shard_map/all_to_all | solution.py:42
  305.8 0.4 fusion.24
  306.2 5.9 %all-to-all-done.3 = bf16[192,1,4,128]{3,0,1,2:T(8,128)(2,1)S(1)} async-done(((bf16[192,1,4,128]{3,0,1,2:T(8,128)(2,1)}), bf16[192,1,4,128]{3,0,1,2:T(8,128)(2,1)S(1)}, u32[]{:S(2)}, u32[]{:S(2)}) %all-to-all-start.3) | async-done | bytes 196640 | tf_op jit(solution)/shard_map/all_to_all | solution.py:42
  312.1 0.4 fusion.25
  312.5 0.7 pad_maximum_fusion
  (38 shorter events, 1.3 us)
Async XLA Ops:
  6.5 63.9 %all-gather.3.cloned.1.call-start = ((), (), s32[]{:S(2)}) async-start(), calls=%async_computation.6 | async-start | bytes 6488064 | tf_op jit(solution)/shard_map/all_gather | solution.py:30
  20.7 100.2 %all-gather.5.cloned.1.call-start = ((), (), s32[]{:S(2)}) async-start(), calls=%async_computation.7 | async-start | bytes 6488064 | tf_op jit(solution)/shard_map/all_gather | solution.py:30
  31.9 178.0 %reduce-scatter.7.cloned.1.call-start = ((), (), s32[]{:S(2)}) async-start(), calls=%async_computation.8 | async-start | bytes 6488064
  70.5 8.2 %copy-start.1 = (bf16[512,6144]{0,1:T(8,128)(2,1)S(1)}, bf16[512,6144]{0,1:T(8,128)(2,1)}, u32[]{:S(2)}) copy-start(bf16[512,6144]{0,1:T(8,128)(2,1)} %all-gather.3.cloned.1.call-done) | copy-start | bytes 18874372
  70.5 14.7 %slice-start = ((s8[6291456]{0:T(1024)(128)(4,1)}), s8[4194304]{0:T(1024)(128)(4,1)S(1)}, s32[]{:S(2)}) async-start(s8[6291456]{0:T(1024)(128)(4,1)} %bitcast.111), calls=%async_computation.10 | async-start | bytes 8388608
  78.7 6.5 %slice-start.1 = ((s8[6291456]{0:T(1024)(128)(4,1)}), s8[2097152]{0:T(1024)(128)(4,1)S(1)}, s32[]{:S(2)}) async-start(s8[6291456]{0:T(1024)(128)(4,1)} %bitcast.111), calls=%async_computation.11 | async-start | bytes 4194304
  99.2 200.4 %reduce-scatter.9.cloned.1.call-start = ((), (), s32[]{:S(2)}) async-start(), calls=%async_computation.9 | async-start | bytes 6488064
  120.9 8.2 %copy-start.2 = (bf16[512,6144]{0,1:T(8,128)(2,1)S(1)}, bf16[512,6144]{0,1:T(8,128)(2,1)}, u32[]{:S(2)}) copy-start(bf16[512,6144]{0,1:T(8,128)(2,1)} %all-gather.5.cloned.1.call-done) | copy-start | bytes 18874372
  120.9 14.8 %slice-start.2 = ((s8[6291456]{0:T(1024)(128)(4,1)}), s8[4194304]{0:T(1024)(128)(4,1)S(1)}, s32[]{:S(2)}) async-start(s8[6291456]{0:T(1024)(128)(4,1)} %bitcast.113), calls=%async_computation.12 | async-start | bytes 8388608
  129.1 6.6 %slice-start.3 = ((s8[6291456]{0:T(1024)(128)(4,1)}), s8[2097152]{0:T(1024)(128)(4,1)S(1)}, s32[]{:S(2)}) async-start(s8[6291456]{0:T(1024)(128)(4,1)} %bitcast.113), calls=%async_computation.13 | async-start | bytes 4194304
  149.8 0.7 copy-start
  211.8 89.7 %all-to-all-start.1 = ((bf16[192,1,4,128]{3,0,1,2:T(8,128)(2,1)}), bf16[192,1,4,128]{3,0,1,2:T(8,128)(2,1)S(1)}, u32[]{:S(2)}, u32[]{:S(2)}) async-start(bf16[192,1,4,128]{3,0,1,2:T(8,128)(2,1)} %copy.25), calls=%async_computation.1 | async-start | bytes 393216 | tf_op jit(solution)/shard_map/all_to_all | solution.py:42
  301.5 10.6 %all-to-all-start.3 = ((bf16[192,1,4,128]{3,0,1,2:T(8,128)(2,1)}), bf16[192,1,4,128]{3,0,1,2:T(8,128)(2,1)S(1)}, u32[]{:S(2)}, u32[]{:S(2)}) async-start(bf16[192,1,4,128]{3,0,1,2:T(8,128)(2,1)} %copy.30), calls=%async_computation.3 | async-start | bytes 393216 | tf_op jit(solution)/shard_map/all_to_all | solution.py:42
Sparse Core Ops, SparseCore 0:
  20.8 49.6 all-gather.2
  72.7 48.1 all-gather.4
  124.6 85.2 reduce-scatter.6
  214.0 85.6 reduce-scatter.8
where the time goes:
time: 321 us; the launch traced here: 320 us
  waiting for transfers between devices  209 us (65%)
  matrix products  43.1 us (13%)
  local copies, waits for them, and re-layouts  24.7 us (8%)
  blocking collectives  19.4 us (6%)
  between operations  13.3 us (4%)
  starting transfers between devices  8.87 us (3%)
    unnamed x6, waiting for transfers between devices  143 us
    all_gather x2, waiting for transfers between devices, expert_layer(): fragment = lax.all_gather(slot_rows, 'blk', axis=1, tiled=True)  60 us
    unnamed x20, local copies, waits for them, and re-layouts  21.7 us
    all_to_all x2, blocking collectives, expert_layer(): lax.all_to_all(outgoing, 'expert', split_axis=1, concat_axis=1, tiled=True)  19.4 us
    dot_general x2, matrix products, expert_layer(): gate_pre = jnp.dot(fragment, gate_mat, preferred_element_type=jnp.float32)  16.4 us
    dot_general x2, matrix products, expert_layer(): up_pre = jnp.dot(fragment, up_mat, preferred_element_type=jnp.float32)  13.1 us
    dot_general x2, matrix products, expert_layer(): lax.dot_general(down_mat, hidden, (((0,), (1,)), ((), ())), preferred_ele...  10.6 us
    all_to_all x2, starting transfers between devices, expert_layer(): lax.all_to_all(summed.reshape(feature_cols, step_count, experts, row_coun...  8.56 us
  transfers between devices with their start and end apart: 6, of which 5 were waited for; matrix products, arithmetic and copies ran while one was open for 20% of the time, Pallas kernels for 0%

commit v1 on v0

--- a/solution.py
+++ b/solution.py
@@ -2,6 +2,11 @@
 import jax.numpy as jnp
 from jax import lax
 from jax.sharding import PartitionSpec as P
+
+
+def all_by_exchange(x, mesh_axis, d):
+    outgoing = jnp.stack([x] * lax.axis_size(mesh_axis))
+    return jnp.concatenate(lax.all_to_all(outgoing, mesh_axis, 0, 0), axis=d)
 
 
 def routing(expert_ids, route_share, experts):
@@ -27,7 +32,7 @@
     ).astype(jnp.bfloat16)
     arrived = lax.all_to_all(outgoing, "expert", split_axis=1, concat_axis=1, tiled=True)
     slot_rows = arrived.reshape(-1, feature_cols)
-    fragment = lax.all_gather(slot_rows, "blk", axis=1, tiled=True)
+    fragment = all_by_exchange(slot_rows, "blk", 1)
     gate_pre = jnp.dot(fragment, gate_mat, preferred_element_type=jnp.float32)
     up_pre = jnp.dot(fragment, up_mat, preferred_element_type=jnp.float32)
     hidden = (jax.nn.silu(gate_pre) * up_pre).astype(jnp.bfloat16)

time: 321 us -> 370 us (1.15)
  blocking collectives: 19.4 us -> 109 us
  waiting for transfers between devices: 209 us -> 165 us
  matrix products: 43.1 us -> 35.9 us
  starting transfers between devices: 8.87 us -> 16 us
    all_to_all x0 -> x1, blocking collectives: none -> 89.7 us  [all_by_exchange(): return jnp.concatenate(lax.all_to_all(outgoing, mesh_axis, 0, 0), axis=d)]
    all_to_all x0 -> x1, waiting for transfers between devices: none -> 77.7 us  [all_by_exchange(): return jnp.concatenate(lax.all_to_all(outgoing, mesh_axis, 0, 0), axis=d)]
    unnamed x6 -> x4, waiting for transfers between devices: 143 us -> 81.2 us
    all_gather x2 -> x0, waiting for transfers between devices: 60 us -> none  [expert_layer(): fragment = lax.all_gather(slot_rows, 'blk', axis=1, tiled=True)]
    all_to_all x0 -> x1, starting transfers between devices: none -> 8.27 us  [all_by_exchange(): return jnp.concatenate(lax.all_to_all(outgoing, mesh_axis, 0, 0), axis=d)]
    dot_general x2, matrix products: 16.4 us -> 11.1 us  [expert_layer(): gate_pre = jnp.dot(fragment, gate_mat, preferred_element_type=jnp.float32)]
    another operation x0 -> x2, local copies, waits for them, and re-layouts: none -> 4.04 us  [all_by_exchange(): outgoing = jnp.stack([x] * lax.axis_size(mesh_axis))]
    unnamed x20 -> x26, local copies, waits for them, and re-layouts: 21.7 us -> 20.8 us
  transfers between devices with their start and end apart: 6 -> 5, of which waited for: 5 -> 3; matrix products, arithmetic and copies ran while one was open for 20% -> 7% of each run, Pallas kernels for 0% -> 0%
where the time goes in v1:
time: 370 us; the launch traced here: 369 us
  waiting for transfers between devices  165 us (45%)
  blocking collectives  109 us (29%)
  matrix products  35.9 us (10%)
  local copies, waits for them, and re-layouts  27.9 us (8%)
  starting transfers between devices  16 us (4%)
  between operations  13.7 us (4%)
    all_to_all x1, blocking collectives, all_by_exchange(): return jnp.concatenate(lax.all_to_all(outgoing, mesh_axis, 0, 0), axis=d)  89.7 us
    unnamed x4, waiting for transfers between devices  81.2 us
    all_to_all x1, waiting for transfers between devices, all_by_exchange(): return jnp.concatenate(lax.all_to_all(outgoing, mesh_axis, 0, 0), axis=d)  77.7 us
    unnamed x26, local copies, waits for them, and re-layouts  20.8 us
    all_to_all x2, blocking collectives, expert_layer(): lax.all_to_all(outgoing, 'expert', split_axis=1, concat_axis=1, tiled=True)  19.4 us
    dot_general x2, matrix products, expert_layer(): up_pre = jnp.dot(fragment, up_mat, preferred_element_type=jnp.float32)  11.8 us
    dot_general x2, matrix products, expert_layer(): gate_pre = jnp.dot(fragment, gate_mat, preferred_element_type=jnp.float32)  11.1 us
    dot_general x2, matrix products, expert_layer(): lax.dot_general(down_mat, hidden, (((0,), (1,)), ((), ())), preferred_ele...  10.7 us
  transfers between devices with their start and end apart: 5, of which 3 were waited for; matrix products, arithmetic and copies ran while one was open for 7% of the time, Pallas kernels for 0%

profile of v1, /device:TPU:0, one launch (start us, length us, event | category | flops | bytes accessed | tf_op | source)
XLA Modules:
  0.0 368.7 jit_solution(3311191771884708615)
XLA Ops:
  6.5 0.8 slice_bitcast_fusion.5
  7.6 0.2 reduce_window_sum.17
  7.9 1.2 fusion.26
  9.1 10.7 %all_to_all.30 = bf16[1,4,128,192]{2,3,0,1:T(8,128)(2,1)S(1)} all-to-all(bf16[1,4,128,192]{2,3,0,1:T(8,128)(2,1)S(1)} %fusion.26), channel_id=1, replica_groups=mesh['expert'=4,'blk'=32] {'expert'}, dimensions={1} | all-to-all | bytes 393216 | tf_op jit(solution)/shard_map/all_to_all | solution.py:33
  20.0 3.3 stack.6
  23.3 8.3 %all-to-all-start.1 = ((bf16[32,512,192]{1,2,0:T(8,128)(2,1)}), bf16[32,512,192]{1,2,0:T(8,128)(2,1)}, u32[]{:S(2)}, u32[]{:S(2)}) async-start(bf16[32,512,192]{1,2,0:T(8,128)(2,1)} %stack.6), calls=%async_computation.1 | async-start | bytes 12582912 | tf_op jit(solution)/shard_map/all_to_all | solution.py:9
  31.9 77.7 %all-to-all-done.1 = bf16[32,512,192]{1,2,0:T(8,128)(2,1)} async-done(((bf16[32,512,192]{1,2,0:T(8,128)(2,1)}), bf16[32,512,192]{1,2,0:T(8,128)(2,1)}, u32[]{:S(2)}, u32[]{:S(2)}) %all-to-all-start.1) | async-done | bytes 6291488 | tf_op jit(solution)/shard_map/all_to_all | solution.py:9
  109.5 7.6 %fusion.10 = f32[512,512]{1,0:T(8,128)S(1)} fusion(bf16[512,6144]{0,1:T(8,128)(2,1)} %bitcast.10, bf16[1,6144,512]{2,1,0:T(8,128)(2,1)} %param.9), kind=kOutput, calls=%fused_computation.12 | convolution fusion | flops 3221225472 | bytes 13631488 | tf_op jit(solution)/shard_map/dot_general | solution.py:36
  117.2 8.3 %fusion.21 = bf16[512,512]{1,0:T(8,128)(2,1)S(1)} fusion(bf16[512,6144]{0,1:T(8,128)(2,1)} %bitcast.10, bf16[1,6144,512]{2,1,0:T(8,128)(2,1)} %param.10, f32[512,512]{1,0:T(8,128)S(1)} %fusion.10), kind=kOutput, calls=%fused_computation.17 | convolution fusion | flops 3222798336 | bytes 14155776 | tf_op jit(solution)/shard_map/dot_general | solution.py:37
  125.5 5.3 %fusion = bf16[6144,512]{0,1:T(8,128)(2,1)} fusion(bf16[512,512]{1,0:T(8,128)(2,1)S(1)} %fusion.21, bf16[1,512,6144]{2,1,0:T(8,128)(2,1)S(1)} %bitcast.124), kind=kOutput, calls=%fused_computation.2 | convolution fusion | flops 3224371200 | bytes 13107200 | tf_op jit(solution)/shard_map/dot_general | solution.py:40
  130.8 8.7 %copy.31 = bf16[6144,512]{1,0:T(8,128)(2,1)} copy(bf16[6144,512]{0,1:T(8,128)(2,1)} %fusion) | data formatting | bytes 12582912
  139.7 0.6 copy-done
  140.3 0.4 fusion.27
  140.7 8.7 %all_to_all.31 = bf16[1,4,128,192]{2,3,0,1:T(8,128)(2,1)S(1)} all-to-all(bf16[1,4,128,192]{2,3,0,1:T(8,128)(2,1)S(1)} %fusion.27), channel_id=1, replica_groups=mesh['expert'=4,'blk'=32] {'expert'}, dimensions={1} | all-to-all | bytes 393216 | tf_op jit(solution)/shard_map/all_to_all | solution.py:33
  149.6 0.7 stack.7
  150.4 89.7 %all_to_all.32 = bf16[32,512,192]{1,2,0:T(8,128)(2,1)S(1)} all-to-all(bf16[32,512,192]{1,2,0:T(8,128)(2,1)S(1)} %stack.7), channel_id=1, replica_groups=mesh['expert'=4,'blk'=32] {'blk'}, dimensions={0} | all-to-all | bytes 12582912 | tf_op jit(solution)/shard_map/all_to_all | solution.py:9
  240.1 3.4 fusion.8
  243.6 3.5 fusion.18
  247.2 5.4 %fusion.1 = bf16[6144,512]{0,1:T(8,128)(2,1)} fusion(bf16[512,512]{1,0:T(8,128)(2,1)S(1)} %fusion.18, bf16[1,512,6144]{2,1,0:T(8,128)(2,1)S(1)} %bitcast.126), kind=kOutput, calls=%fused_computation.3 | convolution fusion | flops 3224371200 | bytes 13107200 | tf_op jit(solution)/shard_map/dot_general | solution.py:40
  252.5 8.6 %copy.33 = bf16[6144,512]{1,0:T(8,128)(2,1)} copy(bf16[6144,512]{0,1:T(8,128)(2,1)} %fusion.1) | data formatting | bytes 12582912
  261.2 0.7 copy-done.1
  261.9 1.1 copy.32
  263.0 0.8 copy.25
  263.8 3.4 all-to-all-start.2
  267.2 81.1 %reduce-scatter.9.cloned.1.call-done = bf16[192,512]{1,0:T(8,128)(2,1)} async-done(((bf16[6144,512]{1,0:T(8,128)(2,1)}), bf16[192,512]{1,0:T(8,128)(2,1)}) %reduce-scatter.9.cloned.1.call-update) | async-done | bytes 196624
  348.3 1.1 copy.34
  349.4 0.8 copy.30
  350.2 4.3 %all-to-all-start.5 = ((bf16[192,1,4,128]{3,0,1,2:T(8,128)(2,1)}), bf16[192,1,4,128]{3,0,1,2:T(8,128)(2,1)S(1)}, u32[]{:S(2)}, u32[]{:S(2)}) async-start(bf16[192,1,4,128]{3,0,1,2:T(8,128)(2,1)} %copy.30), calls=%async_computation.5 | async-start | bytes 393216 | tf_op jit(solution)/shard_map/all_to_all | solution.py:47
  354.5 0.4 fusion.24
  354.9 5.9 %all-to-all-done.5 = bf16[192,1,4,128]{3,0,1,2:T(8,128)(2,1)S(1)} async-done(((bf16[192,1,4,128]{3,0,1,2:T(8,128)(2,1)}), bf16[192,1,4,128]{3,0,1,2:T(8,128)(2,1)S(1)}, u32[]{:S(2)}, u32[]{:S(2)}) %all-to-all-start.5) | async-done | bytes 196640 | tf_op jit(solution)/shard_map/all_to_all | solution.py:47
  360.8 0.4 fusion.25
  361.2 0.7 pad_maximum_fusion
  (45 shorter events, 1.4 us)
Async XLA Ops:
  23.3 86.2 %all-to-all-start.1 = ((bf16[32,512,192]{1,2,0:T(8,128)(2,1)}), bf16[32,512,192]{1,2,0:T(8,128)(2,1)}, u32[]{:S(2)}, u32[]{:S(2)}) async-start(bf16[32,512,192]{1,2,0:T(8,128)(2,1)} %stack.6), calls=%async_computation.1 | async-start | bytes 12582912 | tf_op jit(solution)/shard_map/all_to_all | solution.py:9
  31.6 230.3 %reduce-scatter.7.cloned.1.call-start = ((), (), s32[]{:S(2)}) async-start(), calls=%async_computation.8 | async-start | bytes 6488064
  109.5 15.9 %slice-start.4 = ((s8[6291456]{0:T(1024)(128)(4,1)}), s8[4194304]{0:T(1024)(128)(4,1)S(1)}, s32[]{:S(2)}) async-start(s8[6291456]{0:T(1024)(128)(4,1)} %bitcast.123), calls=%async_computation.14 | async-start | bytes 8388608
  117.2 8.3 %slice-start.5 = ((s8[6291456]{0:T(1024)(128)(4,1)}), s8[2097152]{0:T(1024)(128)(4,1)S(1)}, s32[]{:S(2)}) async-start(s8[6291456]{0:T(1024)(128)(4,1)} %bitcast.123), calls=%async_computation.15 | async-start | bytes 4194304
  139.5 0.9 copy-start
  139.5 208.8 %reduce-scatter.9.cloned.1.call-start = ((), (), s32[]{:S(2)}) async-start(), calls=%async_computation.9 | async-start | bytes 6488064
  149.6 90.5 %slice-start = ((s8[6291456]{0:T(1024)(128)(4,1)}), s8[4194304]{0:T(1024)(128)(4,1)S(1)}, s32[]{:S(2)}) async-start(s8[6291456]{0:T(1024)(128)(4,1)} %bitcast.119), calls=%async_computation.10 | async-start | bytes 8388608
  150.3 89.8 %slice-start.1 = ((s8[6291456]{0:T(1024)(128)(4,1)}), s8[2097152]{0:T(1024)(128)(4,1)S(1)}, s32[]{:S(2)}) async-start(s8[6291456]{0:T(1024)(128)(4,1)} %bitcast.119), calls=%async_computation.11 | async-start | bytes 4194304
  150.4 93.2 %slice-start.2 = ((s8[6291456]{0:T(1024)(128)(4,1)}), s8[4194304]{0:T(1024)(128)(4,1)S(1)}, s32[]{:S(2)}) async-start(s8[6291456]{0:T(1024)(128)(4,1)} %bitcast.121), calls=%async_computation.12 | async-start | bytes 8388608
  240.1 3.5 slice-start.3
  240.1 7.0 %slice-start.6 = ((s8[6291456]{0:T(1024)(128)(4,1)}), s8[4194304]{0:T(1024)(128)(4,1)S(1)}, s32[]{:S(2)}) async-start(s8[6291456]{0:T(1024)(128)(4,1)} %bitcast.125), calls=%async_computation.16 | async-start | bytes 8388608
  243.6 3.6 slice-start.7
  261.2 0.7 copy-start.1
  263.8 86.4 %all-to-all-start.2 = ((bf16[192,1,4,128]{3,0,1,2:T(8,128)(2,1)}), bf16[192,1,4,128]{3,0,1,2:T(8,128)(2,1)S(1)}, u32[]{:S(2)}, u32[]{:S(2)}) async-start(bf16[192,1,4,128]{3,0,1,2:T(8,128)(2,1)} %copy.25), calls=%async_computation.2 | async-start | bytes 393216 | tf_op jit(solution)/shard_map/all_to_all | solution.py:47
  350.2 10.6 %all-to-all-start.5 = ((bf16[192,1,4,128]{3,0,1,2:T(8,128)(2,1)}), bf16[192,1,4,128]{3,0,1,2:T(8,128)(2,1)S(1)}, u32[]{:S(2)}, u32[]{:S(2)}) async-start(bf16[192,1,4,128]{3,0,1,2:T(8,128)(2,1)} %copy.30), calls=%async_computation.5 | async-start | bytes 393216 | tf_op jit(solution)/shard_map/all_to_all | solution.py:47
Sparse Core Ops, SparseCore 0:
  139.6 118.7 reduce-scatter.6
  262.6 85.6 reduce-scatter.8
